TPU v7x, 32 devices: a whole 2x2x4 slice. The times are simulated.
32 devices in a mesh: aux: 4 (over z), pair: 8 (over y, x, core).
Axes of the slice: x: 2, y: 2, z: 4, core: 2. Of those that a mesh axis runs over, the one named last changes fastest.
Arguments:
- b_three: bfloat16 [4096, 2048], P('pair', 'aux'), may hold values from -0.13183594 to 0.13183594
- metric: bfloat16 [2048, 2048], P(None, 'aux'), may hold values from -1 to 2
- aux_map: int32 [64, 32], P('pair', 'aux'), may hold values 0 or 1
- domains: int32 [80, 4], replicated, may hold values from 0 to 63, as said below
- counts: int32 [80], P('pair'), may hold values from 1 to 4, as said below
Outputs:
- pair_integrals: float32 [80, 256, 256], P('pair', 'aux')
Inputs may be any that keep to these rules, and one draw needn't show every extreme that they name: `domains`: of the 40 slots of the pairs of one index of pair (pairs q * 10 to (q + 1) * 10 - 1), at most 5 name blocks held by one index of pair (blocks o * 8 to (o + 1) * 8 - 1), and exactly 5 for some such index in every draw. `counts`: slots at or past a pair's count are padding.
All inputs are finite; a program needn't handle non-finite values. No bound on the sum of `aux_map` on one device may be relied on, other than what follows from the above.
Results may differ from a plain program's by a relative error of at most 0.00079.
Values may be sent and summed in bfloat16 or wider, within the bound.
A program may use at most 64 MiB of HBM per device.

v0:
```python
import functools

import jax
import jax.numpy as jnp
from jax import lax
from jax.experimental import pallas as pl
from jax.experimental.pallas import tpu as pltpu
from jax.sharding import PartitionSpec as P

MESH = pl.DeviceIdType.MESH


def kernel(n, n_pair, split, b_hbm, metric_hbm, map_ref, dom_ref, out_ref, diag_ref,
           b_raw, b_ref, metric_ref, in_sem, b_all, table, g_send, g_recv, d_own, d_recv,
           r_s, r_r, l_s, l_r, p_s, p_r, f_s, f_r, g_s, g_r, d_s, d_r, g_far, far_out, far_recv, far_send, late_send, late_recv, x_s, x_r, c_s):
    chunks, rows, depth = b_hbm.shape
    pairs, slab, width = out_ref.shape
    slots = dom_ref.shape[0]
    chips = n_pair // 2
    z = lax.axis_index("aux")
    q = lax.axis_index("pair")
    core = lax.rem(q, 2)
    chip = q // 2
    partner = q + 1 - 2 * core
    has_right = z + 1 < n
    has_left = z > 0

    def chip_at(k):
        return lax.rem(chip + k + chips, chips) * 2 + core

    load_b = pltpu.make_async_copy(b_hbm.at[0], b_raw.at[0], in_sem.at[0])
    load_rest = pltpu.make_async_copy(b_hbm.at[1:], b_raw.at[1:], in_sem.at[2])
    load_metric = pltpu.make_async_copy(metric_hbm, metric_ref, in_sem.at[1])
    load_b.start()
    load_rest.start()
    load_metric.start()
    barrier = pltpu.get_barrier_semaphore()
    for near_z, there in ((z + 1, has_right), (z - 1, has_left)):
        @pl.when(there)
        def _():
            pl.semaphore_signal(barrier, inc=1, device_id=(near_z, q), device_id_type=MESH)
    for k in range(1, chips):
        pl.semaphore_signal(barrier, inc=1, device_id=(z, chip_at(k)), device_id_type=MESH)
    pl.semaphore_signal(barrier, inc=1, device_id=(z, partner), device_id_type=MESH)
    aux_blocks = map_ref.shape[1]
    spread_row = lax.broadcasted_iota(jnp.int32, (aux_blocks, depth), 0)
    spread_col = lax.broadcasted_iota(jnp.int32, (aux_blocks, depth), 1) // (depth // aux_blocks)
    keep = jnp.dot(map_ref[...].astype(jnp.float32), (spread_row == spread_col).astype(jnp.float32),
                   preferred_element_type=jnp.float32)
    def mask(c):
        b_ref[c] = (b_raw[c].astype(jnp.float32) * keep[c // split:c // split + 1, :]).astype(b_ref.dtype)
    load_b.wait()
    mask(0)
    pl.semaphore_wait(barrier, chips + has_right.astype(jnp.int32) + has_left.astype(jnp.int32))

    def remote(src, dst, send, recv, device):
        return pltpu.make_async_remote_copy(
            src_ref=src, dst_ref=dst, send_sem=send, recv_sem=recv, device_id=device, device_id_type=MESH)

    def along(h, c, right):
        step = 1 if right else -1
        origin = z - step * h
        send, recv = (r_s, r_r) if right else (l_s, l_r)
        src = b_ref.at[c] if h == 0 else b_all.at[origin, c]
        return remote(src, b_all.at[origin, c], send.at[h, c], recv.at[h, c], (z + step, q))

    def arrival(h, c, right):
        recv = r_r if right else l_r
        origin = z - 1 - h if right else z + 1 + h
        return remote(b_ref.at[c], b_all.at[origin, c], recv.at[h, c], recv.at[h, c], (z, partner))

    def own_chunk(c):
        for right in (True, False):
            @pl.when(has_right if right else has_left)
            def _():
                along(0, c, right).start()

    def relay(h, c):
        for right in (True, False):
            came = z - h >= 0 if right else z + h < n

            @pl.when(came)
            def _():
                arrival(h - 1, c, right).wait_recv()

                if h < n - 1:
                    @pl.when(has_right if right else has_left)
                    def _():
                        along(h, c, right).start()

    def spread(k, c):
        target = partner if k == 0 else chip_at(k)
        return remote(table.at[q, c], table.at[q, c], p_s.at[k, c], p_r.at[k, c], (z, target))

    def forward(k, c):
        origin = chip_at(-k)
        return remote(table.at[origin, c], table.at[origin, c], f_s.at[k, c], f_r.at[k, c], (z, partner))

    def fit(c):
        total = jnp.dot(b_ref[c], metric_ref[pl.ds(pl.multiple_of(z * depth, depth), depth), :],
                        preferred_element_type=jnp.float32)
        for k in range(1, n):
            origin = lax.rem(z + k, n)
            total += jnp.dot(b_all[origin, c],
                             metric_ref[pl.ds(pl.multiple_of(origin * depth, depth), depth), :],
                             preferred_element_type=jnp.float32)
        table[q, c] = total.astype(table.dtype)
        for k in list(range(1, chips)) + [0]:
            spread(k, c).start()

    def pass_on(c):
        for k in range(1, chips):
            spread_in = remote(table.at[chip_at(-k), c], table.at[chip_at(-k), c],
                               p_s.at[k, c], p_r.at[k, c], (z, partner))
            spread_in.wait_recv()
            forward(k, c).start()

    own_chunk(0)
    load_rest.wait()
    for c in range(1, chunks):
        mask(c)
    load_metric.wait()

    def stage(step, carry):
        @pl.when(step + 1 < chunks)
        def _():
            own_chunk(step + 1)
        for h in range(n - 1, 0, -1):
            @pl.when((step + 1 >= h) & (step + 1 - h < chunks))
            def _():
                relay(h, step + 1 - h)

        @pl.when((step + 2 >= n) & (step + 2 - n < chunks))
        def _():
            fit(step + 2 - n)

        @pl.when((step >= n) & (step - n < chunks))
        def _():
            pass_on(step - n)
        return carry

    lax.fori_loop(0, chunks + n, stage, 0)

    def finish(c, carry):
        remote(table.at[partner, c], table.at[partner, c], p_s.at[0, c], p_r.at[0, c],
               (z, partner)).wait_recv()
        for k in range(1, chips):
            origin = chip_at(-k) + 1 - 2 * core
            remote(table.at[origin, c], table.at[origin, c], f_s.at[k, c], f_r.at[k, c],
                   (z, partner)).wait_recv()
        return carry

    lax.fori_loop(0, chunks, finish, 0)

    row_of = lax.broadcasted_iota(jnp.int32, (width, width), 0)
    col_of = lax.broadcasted_iota(jnp.int32, (width, width), 1)

    def gram_copy(k, p):
        return remote(g_send.at[lax.rem(z + k, n), p], g_recv.at[k - 1, p],
                      g_s.at[k - 1, p], g_r.at[k - 1, p], (lax.rem(z + k, n), q))

    paired = n == 4
    is_end = (z == 0) | (z == n - 1)
    is_mid = jnp.logical_not(is_end)
    mate = z + 1 - 2 * lax.rem(z, 2)

    half = width // 2

    def near(p):
        return remote(g_send.at[0, p], g_recv.at[0, p], g_s.at[0, p], g_r.at[0, p], (mate, q))

    def late(p):
        return remote(late_send.at[p], late_recv.at[p], g_s.at[0, p], g_r.at[0, p], (mate, q))

    def to_mid(p):
        return remote(far_out.at[p], far_recv.at[p], x_s.at[p], x_r.at[p], (mate, q))

    def across(j, p):
        return remote(far_send.at[j, p], g_recv.at[1, p], c_s.at[j, p], g_r.at[1, p],
                      (jnp.where(z < 2, 2, 0) + j, q))

    def combine(low):
        def one(p, carry):
            to_mid(p).wait_recv()
            top = far_recv[p, 0:half].astype(jnp.float32)
            bottom = far_recv[p, half:width].astype(jnp.float32)
            parts = (top.T, bottom) if low else (top, bottom.T)
            value = (g_far[p] + jnp.concatenate(parts, axis=1)).astype(far_send.dtype)
            for j in ((1, 0) if low else (0, 1)):
                far_send[j, p] = value[j * slab:(j + 1) * slab]
                across(j, p).start()
            return carry
        lax.fori_loop(0, pairs, one, 0)

    def near_late(p, carry):
        late(p).start()
        return carry

    def gram(p, carry):
        blocks = []
        for s in range(slots):
            name = dom_ref[s, q * pairs + p]
            local = lax.rem(name, chunks // split) * split
            for t in range(split):
                blocks.append(table[name // (chunks // split), local + t])
        stack = jnp.concatenate(blocks, axis=0)
        full = lax.dot_general(stack, stack, (((1,), (1,)), ((), ())), preferred_element_type=jnp.float32)
        d_own[p] = jnp.sum(jnp.where(row_of == col_of, full, 0.0), axis=0, keepdims=True)
        for d in range(n):
            part = full[d * slab:(d + 1) * slab]

            @pl.when(z == d)
            def _():
                out_ref[p] = part

            if not paired:
                @pl.when(z != d)
                def _():
                    g_send[d, p] = part.astype(g_send.dtype)
        if paired:
            for end, low in ((0, True), (3, False)):
                near_cols, far_cols = (slice(0, half), slice(half, width))[::1 if low else -1]
                mid = 1 if low else 2

                @pl.when(z == end)
                def _():
                    far_out[p] = full[:, far_cols].astype(far_out.dtype)
                    late_send[p] = full[mid * slab:(mid + 1) * slab, near_cols].astype(late_send.dtype)
                    to_mid(p).start()

                @pl.when(z == mid)
                def _():
                    g_far[p] = full[far_cols]
                    g_send[0, p] = full[end * slab:(end + 1) * slab].astype(g_send.dtype)
                    near(p).start()
        else:
            for k in range(1, n):
                gram_copy(k, p).start()
        return carry

    lax.fori_loop(0, pairs, gram, 0)

    def diag_copy(k):
        return remote(d_own, d_recv.at[k - 1], d_s.at[k - 1], d_r.at[k - 1], (lax.rem(z + k, n), q))

    for k in range(1, n):
        diag_copy(k).start()
    if paired:
        @pl.when(is_end)
        def _():
            lax.fori_loop(0, pairs, near_late, 0)

        for mid, low in ((1, True), (2, False)):
            @pl.when(z == mid)
            def _():
                combine(low)

    def add(p, carry):
        if paired:
            remote(g_send.at[0, p], g_recv.at[1, p], g_s.at[0, p], g_r.at[1, p], (mate, q)).wait_recv()
            total = out_ref[p] + g_recv[1, p].astype(jnp.float32)

            @pl.when(is_end)
            def _():
                near(p).wait_recv()
                out_ref[p] = total + g_recv[0, p].astype(jnp.float32)

            for mid, low in ((1, True), (2, False)):
                @pl.when(z == mid)
                def _():
                    late(p).wait_recv()
                    parts = (late_recv[p], far_recv[p, mid * slab:(mid + 1) * slab])
                    whole = jnp.concatenate(parts if low else parts[::-1], axis=1)
                    out_ref[p] = total + whole.astype(jnp.float32)
            return carry
        total = out_ref[p]
        for k in range(1, n):
            gram_copy(k, p).wait_recv()
            total += g_recv[k - 1, p].astype(jnp.float32)
        out_ref[p] = total
        return carry

    lax.fori_loop(0, pairs, add, 0)
    for k in range(1, n):
        diag_copy(k).wait_recv()

    diag = d_own[...]
    for k in range(1, n):
        diag += d_recv[k - 1]
    diag_ref[...] = diag

    def drain(c, carry):
        for right in (True, False):
            for h in range(n - 1):
                goes = (has_right & (z - h >= 0)) if right else (has_left & (z + h < n))

                @pl.when(goes)
                def _():
                    along(h, c, right).wait_send()
        for k in range(chips):
            spread(k, c).wait_send()
        for k in range(1, chips):
            forward(k, c).wait_send()
        return carry

    lax.fori_loop(0, chunks, drain, 0)

    def drain_gram(p, carry):
        if paired:
            @pl.when(is_end)
            def _():
                late(p).wait_send()
                to_mid(p).wait_send()

            @pl.when(is_mid)
            def _():
                near(p).wait_send()
                for j in range(2):
                    across(j, p).wait_send()
        else:
            for k in range(1, n):
                gram_copy(k, p).wait_send()
        return carry

    lax.fori_loop(0, pairs, drain_gram, 0)
    for k in range(1, n):
        diag_copy(k).wait_send()


def close_kernel(rows, total_ref, diag_ref, cnt_ref, out_ref):
    pairs, slab, width = out_ref.shape
    slab_row = lax.broadcasted_iota(jnp.int32, (slab, width), 0) + lax.axis_index("aux") * slab
    slab_col = lax.broadcasted_iota(jnp.int32, (slab, width), 1)
    last = jnp.maximum(slab_row, slab_col)

    def close(p, carry):
        value = jnp.where(slab_row == slab_col, diag_ref[p], total_ref[p])
        out_ref[p] = jnp.where(last < cnt_ref[p] * rows, value, 0.0)
        return carry

    lax.fori_loop(0, pairs, close, 0)


def per_device(n, n_pair, b_three, metric, aux_map, domains, counts):
    rows_dev, aux_dev = b_three.shape
    blocks_dev, aux_blocks = aux_map.shape
    width_cw = rows_dev // blocks_dev
    pairs = counts.shape[0]
    slots = domains.shape[1]
    width = slots * width_cw
    slab = width // n
    split = 1
    chunks = blocks_dev * split
    chunk_rows = width_cw // split
    columns = metric.shape[1]
    chips = n_pair // 2
    far_pairs = pairs if n == 4 else 1
    vmem = pl.BlockSpec(memory_space=pltpu.VMEM)
    smem = pl.BlockSpec(memory_space=pltpu.SMEM)
    dma = pltpu.SemaphoreType.DMA
    hbm = pl.BlockSpec(memory_space=pl.ANY)
    total, diag = pl.pallas_call(
        functools.partial(kernel, n, n_pair, split),
        out_shape=(jax.ShapeDtypeStruct((pairs, slab, width), jnp.float32),
                   jax.ShapeDtypeStruct((pairs, 1, width), jnp.float32)),
        in_specs=[hbm, hbm, vmem, smem],
        out_specs=(vmem, vmem),
        scratch_shapes=[
            pltpu.VMEM((chunks, chunk_rows, aux_dev), jnp.bfloat16),
            pltpu.VMEM((chunks, chunk_rows, aux_dev), jnp.bfloat16),
            pltpu.VMEM(metric.shape, jnp.bfloat16),
            dma((3,)),
            pltpu.VMEM((n, chunks, chunk_rows, aux_dev), jnp.bfloat16),
            pltpu.VMEM((n_pair, chunks, chunk_rows, columns), jnp.bfloat16),
            pltpu.VMEM((n, pairs, slab, width), jnp.bfloat16),
            pltpu.VMEM((n - 1, pairs, slab, width), jnp.bfloat16),
            pltpu.VMEM((pairs, 1, width), jnp.float32),
            pltpu.VMEM((n - 1, pairs, 1, width), jnp.float32),
            dma((n - 1, chunks)), dma((n - 1, chunks)),
            dma((n - 1, chunks)), dma((n - 1, chunks)),
            dma((chips, chunks)), dma((chips, chunks)),
            dma((chips, chunks)), dma((chips, chunks)),
            dma((n - 1, pairs)), dma((n - 1, pairs)),
            dma((n - 1,)), dma((n - 1,)),
            pltpu.VMEM((far_pairs, width // 2, width), jnp.float32),
            pltpu.VMEM((far_pairs, width, width // 2), jnp.bfloat16),
            pltpu.VMEM((far_pairs, width, width // 2), jnp.bfloat16),
            pltpu.VMEM((2, far_pairs, slab, width), jnp.bfloat16),
            pltpu.VMEM((far_pairs, slab, width // 2), jnp.bfloat16),
            pltpu.VMEM((far_pairs, slab, width // 2), jnp.bfloat16),
            dma((far_pairs,)), dma((far_pairs,)), dma((2, far_pairs)),
        ],
        compiler_params=pltpu.CompilerParams(
            collective_id=0, has_side_effects=True, vmem_limit_bytes=60 * 1024 * 1024),
    )(b_three.reshape(chunks, chunk_rows, aux_dev), metric, aux_map, domains.T)
    return pl.pallas_call(
        functools.partial(close_kernel, width_cw),
        out_shape=jax.ShapeDtypeStruct((pairs, slab, width), jnp.float32),
        in_specs=[vmem, vmem, smem],
        out_specs=vmem,
    )(total, diag, counts)


def solution(mesh):
    return jax.shard_map(
        functools.partial(per_device, mesh.shape["aux"], mesh.shape["pair"]),
        mesh=mesh,
        in_specs=(P("pair", "aux"), P(None, "aux"), P("pair", "aux"), P(), P("pair")),
        out_specs=P("pair", "aux", None),
        check_vma=False,
    )
```

profile of v0, /device:TPU:0, one launch (start us, length us, event | category | flops | bytes accessed | tf_op | source)
XLA Modules:
  0.0 73.1 jit_solution(17675345337496196336)
XLA Ops:
  0.0 71.0 %shard_map.55 = (f32[10,64,256]{2,1,0:T(8,128)}, f32[10,1,256]{2,1,0:T(1,128)}) custom-call(bf16[8,64,512]{2,1,0:T(8,128)(2,1)} %bitcast.2, bf16[2048,512]{1,0:T(8,128)(2,1)} %metric_hbm.1, s32[8,8]{1,0:T(8,128)} %map_ref.1, s32[4,80]{1,0:T(4,128)} %bitcast.3), custom_call_target="tpu_custom_call" | custom-call | tf_op jit(solution)/shard_map/pallas_call | solution.py:362
  71.0 2.1 %shard_map.56 = f32[10,64,256]{2,1,0:T(8,128)} custom-call(f32[10,64,256]{2,1,0:T(8,128)} %get-tuple-element.7.total_ref, f32[10,1,256]{2,1,0:T(1,128)} %get-tuple-element.8.diag_ref, s32[10]{0:T(128)} %cnt_ref.1), custom_call_target="tpu_custom_call" | custom-call | tf_op jit(solution)/shard_map/pallas_call | solution.py:396
where the time goes:
time: 73.3 us; the launch traced here: 73.1 us
  Pallas kernels  73.1 us (100%)
    pallas_call x1, Pallas kernels, per_device(): pl.pallas_call(functools.partial(kernel, n, n_pair, split), out_shape=(ja...  71 us
    pallas_call x1, Pallas kernels, per_device(): pl.pallas_call(functools.partial(close_kernel, width_cw), out_shape=jax.S...  2.06 us

commit v1 on v0

--- a/solution.py
+++ b/solution.py
@@ -10,9 +10,9 @@
 MESH = pl.DeviceIdType.MESH
 
 
-def kernel(n, n_pair, split, b_hbm, metric_hbm, map_ref, dom_ref, out_ref, diag_ref,
+def line_kernel(n, n_pair, split, b_hbm, metric_hbm, map_ref, dom_ref, out_ref, diag_ref,
            b_raw, b_ref, metric_ref, in_sem, b_all, table, g_send, g_recv, d_own, d_recv,
-           r_s, r_r, l_s, l_r, p_s, p_r, f_s, f_r, g_s, g_r, d_s, d_r, g_far, far_out, far_recv, far_send, late_send, late_recv, x_s, x_r, c_s):
+           r_s, r_r, l_s, l_r, p_s, p_r, f_s, f_r, g_s, g_r, d_s, d_r):
     chunks, rows, depth = b_hbm.shape
     pairs, slab, width = out_ref.shape
     slots = dom_ref.shape[0]
@@ -159,43 +159,6 @@
         return remote(g_send.at[lax.rem(z + k, n), p], g_recv.at[k - 1, p],
                       g_s.at[k - 1, p], g_r.at[k - 1, p], (lax.rem(z + k, n), q))
 
-    paired = n == 4
-    is_end = (z == 0) | (z == n - 1)
-    is_mid = jnp.logical_not(is_end)
-    mate = z + 1 - 2 * lax.rem(z, 2)
-
-    half = width // 2
-
-    def near(p):
-        return remote(g_send.at[0, p], g_recv.at[0, p], g_s.at[0, p], g_r.at[0, p], (mate, q))
-
-    def late(p):
-        return remote(late_send.at[p], late_recv.at[p], g_s.at[0, p], g_r.at[0, p], (mate, q))
-
-    def to_mid(p):
-        return remote(far_out.at[p], far_recv.at[p], x_s.at[p], x_r.at[p], (mate, q))
-
-    def across(j, p):
-        return remote(far_send.at[j, p], g_recv.at[1, p], c_s.at[j, p], g_r.at[1, p],
-                      (jnp.where(z < 2, 2, 0) + j, q))
-
-    def combine(low):
-        def one(p, carry):
-            to_mid(p).wait_recv()
-            top = far_recv[p, 0:half].astype(jnp.float32)
-            bottom = far_recv[p, half:width].astype(jnp.float32)
-            parts = (top.T, bottom) if low else (top, bottom.T)
-            value = (g_far[p] + jnp.concatenate(parts, axis=1)).astype(far_send.dtype)
-            for j in ((1, 0) if low else (0, 1)):
-                far_send[j, p] = value[j * slab:(j + 1) * slab]
-                across(j, p).start()
-            return carry
-        lax.fori_loop(0, pairs, one, 0)
-
-    def near_late(p, carry):
-        late(p).start()
-        return carry
-
     def gram(p, carry):
         blocks = []
         for s in range(slots):
@@ -213,29 +176,11 @@
             def _():
                 out_ref[p] = part
 
-            if not paired:
-                @pl.when(z != d)
-                def _():
-                    g_send[d, p] = part.astype(g_send.dtype)
-        if paired:
-            for end, low in ((0, True), (3, False)):
-                near_cols, far_cols = (slice(0, half), slice(half, width))[::1 if low else -1]
-                mid = 1 if low else 2
-
-                @pl.when(z == end)
-                def _():
-                    far_out[p] = full[:, far_cols].astype(far_out.dtype)
-                    late_send[p] = full[mid * slab:(mid + 1) * slab, near_cols].astype(late_send.dtype)
-                    to_mid(p).start()
-
-                @pl.when(z == mid)
-                def _():
-                    g_far[p] = full[far_cols]
-                    g_send[0, p] = full[end * slab:(end + 1) * slab].astype(g_send.dtype)
-                    near(p).start()
-        else:
-            for k in range(1, n):
-                gram_copy(k, p).start()
+            @pl.when(z != d)
+            def _():
+                g_send[d, p] = part.astype(g_send.dtype)
+        for k in range(1, n):
+            gram_copy(k, p).start()
         return carry
 
     lax.fori_loop(0, pairs, gram, 0)
@@ -245,34 +190,7 @@
 
     for k in range(1, n):
         diag_copy(k).start()
-    if paired:
-        @pl.when(is_end)
-        def _():
-            lax.fori_loop(0, pairs, near_late, 0)
-
-        for mid, low in ((1, True), (2, False)):
-            @pl.when(z == mid)
-            def _():
-                combine(low)
-
     def add(p, carry):
-        if paired:
-            remote(g_send.at[0, p], g_recv.at[1, p], g_s.at[0, p], g_r.at[1, p], (mate, q)).wait_recv()
-            total = out_ref[p] + g_recv[1, p].astype(jnp.float32)
-
-            @pl.when(is_end)
-            def _():
-                near(p).wait_recv()
-                out_ref[p] = total + g_recv[0, p].astype(jnp.float32)
-
-            for mid, low in ((1, True), (2, False)):
-                @pl.when(z == mid)
-                def _():
-                    late(p).wait_recv()
-                    parts = (late_recv[p], far_recv[p, mid * slab:(mid + 1) * slab])
-                    whole = jnp.concatenate(parts if low else parts[::-1], axis=1)
-                    out_ref[p] = total + whole.astype(jnp.float32)
-            return carry
         total = out_ref[p]
         for k in range(1, n):
             gram_copy(k, p).wait_recv()
@@ -306,20 +224,435 @@
     lax.fori_loop(0, chunks, drain, 0)
 
     def drain_gram(p, carry):
-        if paired:
-            @pl.when(is_end)
-            def _():
-                late(p).wait_send()
-                to_mid(p).wait_send()
-
-            @pl.when(is_mid)
-            def _():
-                near(p).wait_send()
-                for j in range(2):
-                    across(j, p).wait_send()
-        else:
-            for k in range(1, n):
-                gram_copy(k, p).wait_send()
+        for k in range(1, n):
+            gram_copy(k, p).wait_send()
+        return carry
+
+    lax.fori_loop(0, pairs, drain_gram, 0)
+    for k in range(1, n):
+        diag_copy(k).wait_send()
+
+
+def box_kernel(n, n_pair, split, b_hbm, metric_hbm, map_ref, dom_ref, out_ref, diag_ref,
+               b_raw, b_ref, metric_ref, in_sem, b_all, table, far_metric, fit_part,
+               m_s, m_r, o_s, o_r, w_s, w_r, y_s, y_r,
+               tp_s, tp_r, tt_s, tt_r, tf_s, tf_r, mp_s, mp_r, mt_s, mt_r, mf_s, mf_r,
+               g_send, g_recv, d_own, d_recv, g_s, g_r, d_s, d_r,
+               g_far, far_out, far_recv, far_send, late_send, late_recv, x_s, x_r, c_s):
+    chunks, rows, depth = b_hbm.shape
+    pairs, slab, width = out_ref.shape
+    slots = dom_ref.shape[0]
+    parts = far_metric.shape[1]
+    z = lax.axis_index("aux")
+    q = lax.axis_index("pair")
+    core = lax.rem(q, 2)
+    chip = q // 2
+    flip = 1 - 2 * core
+    partner = q + flip
+    near_x = (chip + 1 - 2 * lax.rem(chip, 2)) * 2 + core
+    near_y = lax.rem(chip + 2, 4) * 2 + core
+    corner = (lax.rem(chip + 2, 4) + 1 - 2 * lax.rem(chip, 2)) * 2 + core
+    mate = z + 1 - 2 * lax.rem(z, 2)
+    other = n - 1 - z
+    low = z < 2
+    is_end = (z == 0) | (z == n - 1)
+    is_mid = jnp.logical_not(is_end)
+
+    load_b = pltpu.make_async_copy(b_hbm.at[0], b_raw.at[0], in_sem.at[0])
+    load_rest = pltpu.make_async_copy(b_hbm.at[1:], b_raw.at[1:], in_sem.at[2])
+    load_metric = pltpu.make_async_copy(metric_hbm, metric_ref, in_sem.at[1])
+    load_b.start()
+    load_rest.start()
+    load_metric.start()
+    barrier = pltpu.get_barrier_semaphore()
+    for there in ((mate, q), (z, partner), (z, near_x), (z, near_y)):
+        pl.semaphore_signal(barrier, inc=1, device_id=there, device_id_type=MESH)
+
+    @pl.when(is_mid)
+    def _():
+        pl.semaphore_signal(barrier, inc=1, device_id=(other, q), device_id_type=MESH)
+
+    aux_blocks = map_ref.shape[1]
+    spread_row = lax.broadcasted_iota(jnp.int32, (aux_blocks, depth), 0)
+    spread_col = lax.broadcasted_iota(jnp.int32, (aux_blocks, depth), 1) // (depth // aux_blocks)
+    keep = jnp.dot(map_ref[...].astype(jnp.float32), (spread_row == spread_col).astype(jnp.float32),
+                   preferred_element_type=jnp.float32)
+
+    def mask(c):
+        b_ref[c] = (b_raw[c].astype(jnp.float32) * keep[c // split:c // split + 1, :]).astype(b_ref.dtype)
+
+    load_b.wait()
+    mask(0)
+    pl.semaphore_wait(barrier, 4 + is_mid.astype(jnp.int32))
+
+    def remote(src, dst, send, recv, device):
+        return pltpu.make_async_remote_copy(
+            src_ref=src, dst_ref=dst, send_sem=send, recv_sem=recv, device_id=device, device_id_type=MESH)
+
+    def swap(c, origin=None):
+        src = b_ref.at[c]
+        return remote(src, b_all.at[z if origin is None else origin, c], m_s.at[c], m_r.at[c], (mate, q))
+
+    def own(c, origin=None):
+        return remote(b_ref.at[c], b_all.at[z if origin is None else origin, c], o_s.at[0, c], o_r.at[0, c], (other, q))
+
+    def relay(c, origin=None):
+        at = b_all.at[mate if origin is None else origin, c]
+        return remote(at, at, o_s.at[1, c], o_r.at[1, c], (other, q))
+
+    def half_fit(c):
+        return remote(fit_part.at[c], fit_part.at[c], w_s.at[c], w_r.at[c], (mate, q))
+
+    far_first = jnp.where(z == 0, n // 2, 0) * depth
+    piece = parts * rows
+
+    def metric_part(t):
+        start = pl.multiple_of(far_first + q * piece + t * rows, rows)
+        return remote(metric_ref.at[pl.ds(start, rows)], far_metric.at[q, t], y_s.at[t], y_r.at[t], (mate, q))
+
+    def in_plane(buf, p_s, p_r, t_s, t_r, f_s, f_r):
+        half = rows // 2
+
+        def give(k, c):
+            target = (partner, near_x, near_y)[k]
+            return remote(buf.at[q, c], buf.at[q, c], p_s.at[k, c], p_r.at[k, c], (z, target))
+
+        def turn(k, c):
+            at = buf.at[(near_x, near_y)[k], c, pl.ds(k * half, half)]
+            return remote(at, at, t_s.at[k, c], t_r.at[k, c], (z, (near_y, near_x)[k]))
+
+        def forward(k, c):
+            at = buf.at[(near_x, near_y, corner)[k], c]
+            return remote(at, at, f_s.at[k, c], f_r.at[k, c], (z, partner))
+
+        def share(c):
+            for k in (1, 2, 0):
+                give(k, c).start()
+
+        def pass_on(c):
+            for k in (0, 1):
+                at = buf.at[(near_x, near_y)[k], c]
+                remote(at, at, p_s.at[k + 1, c], p_r.at[k + 1, c], (z, partner)).wait_recv()
+                turn(k, c).start()
+                forward(k, c).start()
+
+        def pass_corner(c):
+            for k in (0, 1):
+                at = buf.at[corner, c, pl.ds(k * half, half)]
+                remote(at, at, t_s.at[k, c], t_r.at[k, c], (z, partner)).wait_recv()
+            forward(2, c).start()
+
+        def finish(c):
+            at = buf.at[partner, c]
+            remote(at, at, p_s.at[0, c], p_r.at[0, c], (z, partner)).wait_recv()
+            for k in range(3):
+                at = buf.at[(near_x, near_y, corner)[k] + flip, c]
+                remote(at, at, f_s.at[k, c], f_r.at[k, c], (z, partner)).wait_recv()
+
+        def drain(c):
+            for k in range(3):
+                give(k, c).wait_send()
+                forward(k, c).wait_send()
+            for k in range(2):
+                turn(k, c).wait_send()
+
+        return share, pass_on, pass_corner, finish, drain
+
+    share, pass_on, pass_corner, finish, drain = in_plane(table, tp_s, tp_r, tt_s, tt_r, tf_s, tf_r)
+    m_share, m_pass_on, m_pass_corner, m_finish, m_drain = in_plane(far_metric, mp_s, mp_r, mt_s, mt_r, mf_s, mf_r)
+
+    def metric_rows(origin):
+        return metric_ref[pl.ds(pl.multiple_of(origin * depth, depth), depth), :]
+
+    def arrive(c):
+        own(c, other).wait_recv()
+        relay(c, n - 1 - mate).wait_recv()
+
+    def fit_mid(c):
+        total = jnp.dot(b_ref[c], metric_rows(z), preferred_element_type=jnp.float32)
+        for origin in (mate, other, n - 1 - mate):
+            total += jnp.dot(b_all[origin, c], metric_rows(origin), preferred_element_type=jnp.float32)
+        table[q, c] = total.astype(table.dtype)
+        share(c)
+
+    def fit_far(c):
+        far = jnp.where(low, n // 2, 0)
+        group = 2 * piece
+        per_slice = depth // group
+        total = None
+        for j in range(n // 2 * per_slice):
+            lhs = b_all[far + j // per_slice, c, :, (j % per_slice) * group:(j % per_slice + 1) * group]
+            rhs = jnp.concatenate([far_metric[2 * j + k, t] for k in range(2) for t in range(parts)], axis=0)
+            term = jnp.dot(lhs, rhs, preferred_element_type=jnp.float32)
+            total = term if total is None else total + term
+        fit_part[c] = total.astype(fit_part.dtype)
+        half_fit(c).start()
+
+    def fit_end(c):
+        swap(c, mate).wait_recv()
+        total = jnp.dot(b_ref[c], metric_rows(z), preferred_element_type=jnp.float32)
+        total += jnp.dot(b_all[mate, c], metric_rows(mate), preferred_element_type=jnp.float32)
+        half_fit(c).wait_recv()
+        table[q, c] = (total + fit_part[c].astype(jnp.float32)).astype(table.dtype)
+        share(c)
+
+    @pl.when(is_mid)
+    def _():
+        own(0).start()
+
+    swap(0).start()
+    load_rest.wait()
+    for c in range(1, chunks):
+        mask(c)
+
+        @pl.when(is_mid)
+        def _():
+            if c < 2:
+                own(c).start()
+            swap(c).start()
+
+    load_metric.wait()
+
+    @pl.when(is_end)
+    def _():
+        for c in range(1, chunks):
+            if c <= parts:
+                metric_part(c - 1).start()
+            swap(c).start()
+
+        def stage(c, carry):
+            @pl.when(c < chunks)
+            def _():
+                fit_end(c)
+
+            @pl.when((c >= 1) & (c < chunks + 1))
+            def _():
+                pass_on(c - 1)
+
+            @pl.when(c >= 2)
+            def _():
+                pass_corner(c - 2)
+            return carry
+
+        lax.fori_loop(0, chunks + 2, stage, 0)
+
+    @pl.when(is_mid)
+    def _():
+        ready = parts + 2
+
+        def stage(s, carry):
+            @pl.when(s < chunks)
+            def _():
+                swap(s, mate).wait_recv()
+                relay(s).start()
+
+            @pl.when(s + 2 < chunks)
+            def _():
+                own(s + 2).start()
+
+            @pl.when((s >= 1) & (s <= parts))
+            def _():
+                t = s - 1
+                at = far_metric.at[q, t]
+                remote(at, at, y_s.at[t], y_r.at[t], (z, partner)).wait_recv()
+                m_share(t)
+
+            @pl.when((s >= 2) & (s < parts + 2))
+            def _():
+                m_pass_on(s - 2)
+
+            @pl.when((s >= 3) & (s < parts + 3))
+            def _():
+                m_pass_corner(s - 3)
+
+            @pl.when((s >= 1) & (s <= chunks))
+            def _():
+                arrive(s - 1)
+
+            first = 2 * (s - ready)
+            late_step = first >= s
+
+            @pl.when((s > ready) & late_step & (s <= chunks))
+            def _():
+                fit_far(s - 1)
+
+            @pl.when((s >= 1) & (s <= chunks))
+            def _():
+                fit_mid(s - 1)
+
+            @pl.when((s >= 2) & (s < chunks + 2))
+            def _():
+                pass_on(s - 2)
+
+            @pl.when(s >= 3)
+            def _():
+                pass_corner(s - 3)
+
+            @pl.when(s == ready)
+            def _():
+                for t in range(parts):
+                    m_finish(t)
+
+            @pl.when((s >= ready) & jnp.logical_not(late_step))
+            def _():
+                for c in (first, first + 1):
+                    @pl.when((c < s) & (c < chunks))
+                    def _():
+                        fit_far(c)
+            return carry
+
+        lax.fori_loop(0, chunks + 3, stage, 0)
+
+    def finish_all(c, carry):
+        finish(c)
+        return carry
+
+    lax.fori_loop(0, chunks, finish_all, 0)
+
+    row_of = lax.broadcasted_iota(jnp.int32, (width, width), 0)
+    col_of = lax.broadcasted_iota(jnp.int32, (width, width), 1)
+
+    half = width // 2
+
+    def near(p):
+        return remote(g_send.at[0, p], g_recv.at[0, p], g_s.at[0, p], g_r.at[0, p], (mate, q))
+
+    def late(p):
+        return remote(late_send.at[p], late_recv.at[p], g_s.at[0, p], g_r.at[0, p], (mate, q))
+
+    def to_mid(p):
+        return remote(far_out.at[p], far_recv.at[p], x_s.at[p], x_r.at[p], (mate, q))
+
+    def across(j, p):
+        return remote(far_send.at[j, p], g_recv.at[1, p], c_s.at[j, p], g_r.at[1, p],
+                      (jnp.where(z < 2, 2, 0) + j, q))
+
+    def combine(below):
+        def one(p, carry):
+            to_mid(p).wait_recv()
+            top = far_recv[p, 0:half].astype(jnp.float32)
+            bottom = far_recv[p, half:width].astype(jnp.float32)
+            parts = (top.T, bottom) if below else (top, bottom.T)
+            value = (g_far[p] + jnp.concatenate(parts, axis=1)).astype(far_send.dtype)
+            for j in ((1, 0) if below else (0, 1)):
+                far_send[j, p] = value[j * slab:(j + 1) * slab]
+                across(j, p).start()
+            return carry
+        lax.fori_loop(0, pairs, one, 0)
+
+    def near_late(p, carry):
+        late(p).start()
+        return carry
+
+    def gram(p, carry):
+        blocks = []
+        for s in range(slots):
+            name = dom_ref[s, q * pairs + p]
+            local = lax.rem(name, chunks // split) * split
+            for t in range(split):
+                blocks.append(table[name // (chunks // split), local + t])
+        stack = jnp.concatenate(blocks, axis=0)
+        full = lax.dot_general(stack, stack, (((1,), (1,)), ((), ())), preferred_element_type=jnp.float32)
+        d_own[p] = jnp.sum(jnp.where(row_of == col_of, full, 0.0), axis=0, keepdims=True)
+        for d in range(n):
+            part = full[d * slab:(d + 1) * slab]
+
+            @pl.when(z == d)
+            def _():
+                out_ref[p] = part
+
+        for end, below in ((0, True), (3, False)):
+            near_cols, far_cols = (slice(0, half), slice(half, width))[::1 if below else -1]
+            mid = 1 if below else 2
+
+            @pl.when(z == end)
+            def _():
+                far_out[p] = full[:, far_cols].astype(far_out.dtype)
+                late_send[p] = full[mid * slab:(mid + 1) * slab, near_cols].astype(late_send.dtype)
+                to_mid(p).start()
+
+            @pl.when(z == mid)
+            def _():
+                g_far[p] = full[far_cols]
+                g_send[0, p] = full[end * slab:(end + 1) * slab].astype(g_send.dtype)
+                near(p).start()
+        return carry
+
+    lax.fori_loop(0, pairs, gram, 0)
+
+    def diag_copy(k):
+        return remote(d_own, d_recv.at[k - 1], d_s.at[k - 1], d_r.at[k - 1], (lax.rem(z + k, n), q))
+
+    for k in range(1, n):
+        diag_copy(k).start()
+    @pl.when(is_end)
+    def _():
+        lax.fori_loop(0, pairs, near_late, 0)
+
+    for mid, below in ((1, True), (2, False)):
+        @pl.when(z == mid)
+        def _():
+            combine(below)
+
+    def add(p, carry):
+        remote(g_send.at[0, p], g_recv.at[1, p], g_s.at[0, p], g_r.at[1, p], (mate, q)).wait_recv()
+        total = out_ref[p] + g_recv[1, p].astype(jnp.float32)
+
+        @pl.when(is_end)
+        def _():
+            near(p).wait_recv()
+            out_ref[p] = total + g_recv[0, p].astype(jnp.float32)
+
+        for mid, below in ((1, True), (2, False)):
+            @pl.when(z == mid)
+            def _():
+                late(p).wait_recv()
+                pieces = (late_recv[p], far_recv[p, mid * slab:(mid + 1) * slab])
+                whole = jnp.concatenate(pieces if below else pieces[::-1], axis=1)
+                out_ref[p] = total + whole.astype(jnp.float32)
+        return carry
+
+    lax.fori_loop(0, pairs, add, 0)
+    for k in range(1, n):
+        diag_copy(k).wait_recv()
+
+    diag = d_own[...]
+    for k in range(1, n):
+        diag += d_recv[k - 1]
+    diag_ref[...] = diag
+
+    def drain_all(c, carry):
+        swap(c).wait_send()
+        drain(c)
+
+        @pl.when(is_mid)
+        def _():
+            own(c).wait_send()
+            relay(c).wait_send()
+            half_fit(c).wait_send()
+        return carry
+
+    lax.fori_loop(0, chunks, drain_all, 0)
+    for t in range(parts):
+        @pl.when(is_end)
+        def _():
+            metric_part(t).wait_send()
+
+        @pl.when(is_mid)
+        def _():
+            m_drain(t)
+
+    def drain_gram(p, carry):
+        @pl.when(is_end)
+        def _():
+            late(p).wait_send()
+            to_mid(p).wait_send()
+
+        @pl.when(is_mid)
+        def _():
+            near(p).wait_send()
+            for j in range(2):
+                across(j, p).wait_send()
         return carry
 
     lax.fori_loop(0, pairs, drain_gram, 0)
@@ -354,42 +687,57 @@
     chunk_rows = width_cw // split
     columns = metric.shape[1]
     chips = n_pair // 2
-    far_pairs = pairs if n == 4 else 1
+    box = n == 4 and n_pair == 8
+    parts = n // 2 * aux_dev // (n_pair * chunk_rows)
     vmem = pl.BlockSpec(memory_space=pltpu.VMEM)
     smem = pl.BlockSpec(memory_space=pltpu.SMEM)
     dma = pltpu.SemaphoreType.DMA
     hbm = pl.BlockSpec(memory_space=pl.ANY)
+    bf16 = jnp.bfloat16
+    scratch = [
+        pltpu.VMEM((chunks, chunk_rows, aux_dev), bf16),
+        pltpu.VMEM((chunks, chunk_rows, aux_dev), bf16),
+        pltpu.VMEM(metric.shape, bf16),
+        dma((3,)),
+        pltpu.VMEM((n, chunks, chunk_rows, aux_dev), bf16),
+        pltpu.VMEM((n_pair, chunks, chunk_rows, columns), bf16),
+    ]
+    grams = [
+        pltpu.VMEM((1 if box else n, pairs, slab, width), bf16),
+        pltpu.VMEM((2 if box else n - 1, pairs, slab, width), bf16),
+        pltpu.VMEM((pairs, 1, width), jnp.float32),
+        pltpu.VMEM((n - 1, pairs, 1, width), jnp.float32),
+    ]
+    gram_sems = [dma((n - 1, pairs)), dma((n - 1, pairs)), dma((n - 1,)), dma((n - 1,))]
+    if box:
+        body = box_kernel
+        scratch += [
+            pltpu.VMEM((n_pair, parts, chunk_rows, columns), bf16),
+            pltpu.VMEM((chunks, chunk_rows, columns), bf16),
+            dma((chunks,)), dma((chunks,)), dma((2, chunks)), dma((2, chunks)),
+            dma((chunks,)), dma((chunks,)), dma((parts,)), dma((parts,)),
+        ]
+        for count in (chunks, parts):
+            scratch += [dma((k, count)) for k in (3, 3, 2, 2, 3, 3)]
+        scratch += grams + gram_sems + [
+            pltpu.VMEM((pairs, width // 2, width), jnp.float32),
+            pltpu.VMEM((pairs, width, width // 2), bf16),
+            pltpu.VMEM((pairs, width, width // 2), bf16),
+            pltpu.VMEM((2, pairs, slab, width), bf16),
+            pltpu.VMEM((pairs, slab, width // 2), bf16),
+            pltpu.VMEM((pairs, slab, width // 2), bf16),
+            dma((pairs,)), dma((pairs,)), dma((2, pairs)),
+        ]
+    else:
+        body = line_kernel
+        scratch += grams + [dma((n - 1, chunks)) for _ in range(4)] + [dma((chips, chunks)) for _ in range(4)] + gram_sems
     total, diag = pl.pallas_call(
-        functools.partial(kernel, n, n_pair, split),
+        functools.partial(body, n, n_pair, split),
         out_shape=(jax.ShapeDtypeStruct((pairs, slab, width), jnp.float32),
                    jax.ShapeDtypeStruct((pairs, 1, width), jnp.float32)),
         in_specs=[hbm, hbm, vmem, smem],
         out_specs=(vmem, vmem),
-        scratch_shapes=[
-            pltpu.VMEM((chunks, chunk_rows, aux_dev), jnp.bfloat16),
-            pltpu.VMEM((chunks, chunk_rows, aux_dev), jnp.bfloat16),
-            pltpu.VMEM(metric.shape, jnp.bfloat16),
-            dma((3,)),
-            pltpu.VMEM((n, chunks, chunk_rows, aux_dev), jnp.bfloat16),
-            pltpu.VMEM((n_pair, chunks, chunk_rows, columns), jnp.bfloat16),
-            pltpu.VMEM((n, pairs, slab, width), jnp.bfloat16),
-            pltpu.VMEM((n - 1, pairs, slab, width), jnp.bfloat16),
-            pltpu.VMEM((pairs, 1, width), jnp.float32),
-            pltpu.VMEM((n - 1, pairs, 1, width), jnp.float32),
-            dma((n - 1, chunks)), dma((n - 1, chunks)),
-            dma((n - 1, chunks)), dma((n - 1, chunks)),
-            dma((chips, chunks)), dma((chips, chunks)),
-            dma((chips, chunks)), dma((chips, chunks)),
-            dma((n - 1, pairs)), dma((n - 1, pairs)),
-            dma((n - 1,)), dma((n - 1,)),
-            pltpu.VMEM((far_pairs, width // 2, width), jnp.float32),
-            pltpu.VMEM((far_pairs, width, width // 2), jnp.bfloat16),
-            pltpu.VMEM((far_pairs, width, width // 2), jnp.bfloat16),
-            pltpu.VMEM((2, far_pairs, slab, width), jnp.bfloat16),
-            pltpu.VMEM((far_pairs, slab, width // 2), jnp.bfloat16),
-            pltpu.VMEM((far_pairs, slab, width // 2), jnp.bfloat16),
-            dma((far_pairs,)), dma((far_pairs,)), dma((2, far_pairs)),
-        ],
+        scratch_shapes=scratch,
         compiler_params=pltpu.CompilerParams(
             collective_id=0, has_side_effects=True, vmem_limit_bytes=60 * 1024 * 1024),
     )(b_three.reshape(chunks, chunk_rows, aux_dev), metric, aux_map, domains.T)

time: 73.3 us -> 78.3 us (1.068)
  Pallas kernels: 73.1 us -> 78 us
    pallas_call x1, Pallas kernels: 71 us -> 76 us  [per_device(): pl.pallas_call(functools.partial(body, n, n_pair, split), out_shape=(jax....]
where the time goes in v1:
time: 78.3 us; the launch traced here: 78.1 us
  Pallas kernels  78 us (100%)
    pallas_call x1, Pallas kernels, per_device(): pl.pallas_call(functools.partial(body, n, n_pair, split), out_shape=(jax....  76 us
    pallas_call x1, Pallas kernels, per_device(): pl.pallas_call(functools.partial(close_kernel, width_cw), out_shape=jax.S...  2.06 us

profile of v1, /device:TPU:0, one launch (start us, length us, event | category | flops | bytes accessed | tf_op | source)
XLA Modules:
  0.0 78.1 jit_solution(1666745602834226869)
XLA Ops:
  0.0 76.0 %shard_map.55 = (f32[10,64,256]{2,1,0:T(8,128)}, f32[10,1,256]{2,1,0:T(1,128)}) custom-call(bf16[8,64,512]{2,1,0:T(8,128)(2,1)} %bitcast.2, bf16[2048,512]{1,0:T(8,128)(2,1)} %metric_hbm.1, s32[8,8]{1,0:T(8,128)} %map_ref.1, s32[4,80]{1,0:T(4,128)} %bitcast.3), custom_call_target="tpu_custom_call" | custom-call | tf_op jit(solution)/shard_map/pallas_call | solution.py:734
  76.0 2.1 %shard_map.56 = f32[10,64,256]{2,1,0:T(8,128)} custom-call(f32[10,64,256]{2,1,0:T(8,128)} %get-tuple-element.7.total_ref, f32[10,1,256]{2,1,0:T(1,128)} %get-tuple-element.8.diag_ref, s32[10]{0:T(128)} %cnt_ref.1), custom_call_target="tpu_custom_call" | custom-call | tf_op jit(solution)/shard_map/pallas_call | solution.py:744

commit v2 on v1

--- a/solution.py
+++ b/solution.py
@@ -234,8 +234,8 @@
 
 
 def box_kernel(n, n_pair, split, b_hbm, metric_hbm, map_ref, dom_ref, out_ref, diag_ref,
-               b_raw, b_ref, metric_ref, in_sem, b_all, table, far_metric, fit_part,
-               m_s, m_r, o_s, o_r, w_s, w_r, y_s, y_r,
+               b_raw, metric_ref, in_sem, b_all, table, far_metric, fit_part,
+               m_s, m_r, o_s, o_r, raw_s, raw_r, w_s, w_r, y_s, y_r,
                tp_s, tp_r, tt_s, tt_r, tf_s, tf_r, mp_s, mp_r, mt_s, mt_r, mf_s, mf_r,
                g_send, g_recv, d_own, d_recv, g_s, g_r, d_s, d_r,
                g_far, far_out, far_recv, far_send, late_send, late_recv, x_s, x_r, c_s):
@@ -279,7 +279,7 @@
                    preferred_element_type=jnp.float32)
 
     def mask(c):
-        b_ref[c] = (b_raw[c].astype(jnp.float32) * keep[c // split:c // split + 1, :]).astype(b_ref.dtype)
+        b_all[z, c] = (b_raw[c].astype(jnp.float32) * keep[c // split:c // split + 1, :]).astype(b_all.dtype)
 
     load_b.wait()
     mask(0)
@@ -290,20 +290,29 @@
             src_ref=src, dst_ref=dst, send_sem=send, recv_sem=recv, device_id=device, device_id_type=MESH)
 
     def swap(c, origin=None):
-        src = b_ref.at[c]
-        return remote(src, b_all.at[z if origin is None else origin, c], m_s.at[c], m_r.at[c], (mate, q))
+        at = b_all.at[z if origin is None else origin, c]
+        return remote(at, at, m_s.at[c], m_r.at[c], (mate, q))
 
     def own(c, origin=None):
-        return remote(b_ref.at[c], b_all.at[z if origin is None else origin, c], o_s.at[0, c], o_r.at[0, c], (other, q))
+        at = b_all.at[z if origin is None else origin, c]
+        return remote(at, at, o_s.at[0, c], o_r.at[0, c], (other, q))
 
     def relay(c, origin=None):
         at = b_all.at[mate if origin is None else origin, c]
         return remote(at, at, o_s.at[1, c], o_r.at[1, c], (other, q))
 
+    def raw(k, c):
+        at = b_all.at[other if k == 0 else n - 1 - mate, c]
+        return remote(at, at, raw_s.at[k, c], raw_r.at[k, c], (mate, q))
+
+    def raw_in(k, c):
+        at = b_all.at[n - 1 - mate if k == 0 else other, c]
+        return remote(at, at, raw_s.at[k, c], raw_r.at[k, c], (mate, q))
+
     def half_fit(c):
         return remote(fit_part.at[c], fit_part.at[c], w_s.at[c], w_r.at[c], (mate, q))
 
-    far_first = jnp.where(z == 0, n // 2, 0) * depth
+    far_first = jnp.where(z == 0, depth, 0)
     piece = parts * rows
 
     def metric_part(t):
@@ -361,6 +370,8 @@
     share, pass_on, pass_corner, finish, drain = in_plane(table, tp_s, tp_r, tt_s, tt_r, tf_s, tf_r)
     m_share, m_pass_on, m_pass_corner, m_finish, m_drain = in_plane(far_metric, mp_s, mp_r, mt_s, mt_r, mf_s, mf_r)
 
+    whole = parts + 1
+
     def metric_rows(origin):
         return metric_ref[pl.ds(pl.multiple_of(origin * depth, depth), depth), :]
 
@@ -368,30 +379,28 @@
         own(c, other).wait_recv()
         relay(c, n - 1 - mate).wait_recv()
 
-    def fit_mid(c):
-        total = jnp.dot(b_ref[c], metric_rows(z), preferred_element_type=jnp.float32)
-        for origin in (mate, other, n - 1 - mate):
+    def fit(c):
+        total = jnp.dot(b_all[z, c], metric_rows(z), preferred_element_type=jnp.float32)
+        for k in range(1, n):
+            origin = lax.rem(z + k, n)
             total += jnp.dot(b_all[origin, c], metric_rows(origin), preferred_element_type=jnp.float32)
         table[q, c] = total.astype(table.dtype)
         share(c)
 
     def fit_far(c):
-        far = jnp.where(low, n // 2, 0)
-        group = 2 * piece
-        per_slice = depth // group
+        first = jnp.where(low, 1, 0)
+        tiles = depth // rows // 2
         total = None
-        for j in range(n // 2 * per_slice):
-            lhs = b_all[far + j // per_slice, c, :, (j % per_slice) * group:(j % per_slice + 1) * group]
-            rhs = jnp.concatenate([far_metric[2 * j + k, t] for k in range(2) for t in range(parts)], axis=0)
+        for j in range(2 * (n - 1)):
+            lhs = b_all[first + j // 2, c, :, (j % 2) * tiles * rows:(j % 2 + 1) * tiles * rows]
+            rhs = jnp.concatenate([far_metric[u // parts, u % parts] for u in range(j * tiles, (j + 1) * tiles)], axis=0)
             term = jnp.dot(lhs, rhs, preferred_element_type=jnp.float32)
             total = term if total is None else total + term
         fit_part[c] = total.astype(fit_part.dtype)
         half_fit(c).start()
 
     def fit_end(c):
-        swap(c, mate).wait_recv()
-        total = jnp.dot(b_ref[c], metric_rows(z), preferred_element_type=jnp.float32)
-        total += jnp.dot(b_all[mate, c], metric_rows(mate), preferred_element_type=jnp.float32)
+        total = jnp.dot(b_all[z, c], metric_rows(z), preferred_element_type=jnp.float32)
         half_fit(c).wait_recv()
         table[q, c] = (total + fit_part[c].astype(jnp.float32)).astype(table.dtype)
         share(c)
@@ -409,7 +418,8 @@
         def _():
             if c < 2:
                 own(c).start()
-            swap(c).start()
+            if c < whole:
+                swap(c).start()
 
     load_metric.wait()
 
@@ -421,35 +431,31 @@
             swap(c).start()
 
         def stage(c, carry):
-            @pl.when(c < chunks)
+            @pl.when(c < whole)
+            def _():
+                swap(c, mate).wait_recv()
+                for k in (0, 1):
+                    raw_in(k, c).wait_recv()
+                fit(c)
+
+            @pl.when((c >= whole) & (c < chunks))
             def _():
                 fit_end(c)
 
-            @pl.when((c >= 1) & (c < chunks + 1))
-            def _():
-                pass_on(c - 1)
-
-            @pl.when(c >= 2)
-            def _():
-                pass_corner(c - 2)
+            @pl.when((c >= 2) & (c < chunks + 2))
+            def _():
+                pass_on(c - 2)
+
+            @pl.when(c >= 4)
+            def _():
+                pass_corner(c - 4)
             return carry
 
-        lax.fori_loop(0, chunks + 2, stage, 0)
+        lax.fori_loop(0, chunks + 4, stage, 0)
 
     @pl.when(is_mid)
     def _():
-        ready = parts + 2
-
         def stage(s, carry):
-            @pl.when(s < chunks)
-            def _():
-                swap(s, mate).wait_recv()
-                relay(s).start()
-
-            @pl.when(s + 2 < chunks)
-            def _():
-                own(s + 2).start()
-
             @pl.when((s >= 1) & (s <= parts))
             def _():
                 t = s - 1
@@ -457,6 +463,15 @@
                 remote(at, at, y_s.at[t], y_r.at[t], (z, partner)).wait_recv()
                 m_share(t)
 
+            @pl.when(s < chunks)
+            def _():
+                swap(s, mate).wait_recv()
+                relay(s).start()
+
+            @pl.when(s + 2 < chunks)
+            def _():
+                own(s + 2).start()
+
             @pl.when((s >= 2) & (s < parts + 2))
             def _():
                 m_pass_on(s - 2)
@@ -465,43 +480,43 @@
             def _():
                 m_pass_corner(s - 3)
 
-            @pl.when((s >= 1) & (s <= chunks))
-            def _():
-                arrive(s - 1)
-
-            first = 2 * (s - ready)
-            late_step = first >= s
-
-            @pl.when((s > ready) & late_step & (s <= chunks))
-            def _():
-                fit_far(s - 1)
-
-            @pl.when((s >= 1) & (s <= chunks))
-            def _():
-                fit_mid(s - 1)
-
-            @pl.when((s >= 2) & (s < chunks + 2))
-            def _():
-                pass_on(s - 2)
-
-            @pl.when(s >= 3)
-            def _():
-                pass_corner(s - 3)
-
-            @pl.when(s == ready)
+            c = s - 2
+            inside = (c >= 0) & (c < chunks)
+
+            @pl.when(inside)
+            def _():
+                own(c, other).wait_recv()
+                relay(c, n - 1 - mate).wait_recv()
+
+            @pl.when(inside & (c < whole))
+            def _():
+                for k in (0, 1):
+                    raw(k, c).start()
+
+            @pl.when(inside & (c > whole))
+            def _():
+                fit_far(c)
+
+            @pl.when(inside)
+            def _():
+                fit(c)
+
+            @pl.when(c == whole)
             def _():
                 for t in range(parts):
                     m_finish(t)
-
-            @pl.when((s >= ready) & jnp.logical_not(late_step))
-            def _():
-                for c in (first, first + 1):
-                    @pl.when((c < s) & (c < chunks))
-                    def _():
-                        fit_far(c)
+                fit_far(c)
+
+            @pl.when((s >= 4) & (s < chunks + 4))
+            def _():
+                pass_on(s - 4)
+
+            @pl.when(s >= 6)
+            def _():
+                pass_corner(s - 6)
             return carry
 
-        lax.fori_loop(0, chunks + 3, stage, 0)
+        lax.fori_loop(0, chunks + 6, stage, 0)
 
     def finish_all(c, carry):
         finish(c)
@@ -622,14 +637,25 @@
     diag_ref[...] = diag
 
     def drain_all(c, carry):
-        swap(c).wait_send()
         drain(c)
+
+        @pl.when(is_end | (c < whole))
+        def _():
+            swap(c).wait_send()
 
         @pl.when(is_mid)
         def _():
             own(c).wait_send()
             relay(c).wait_send()
-            half_fit(c).wait_send()
+
+            @pl.when(c < whole)
+            def _():
+                for k in (0, 1):
+                    raw(k, c).wait_send()
+
+            @pl.when(c >= whole)
+            def _():
+                half_fit(c).wait_send()
         return carry
 
     lax.fori_loop(0, chunks, drain_all, 0)
@@ -688,15 +714,13 @@
     columns = metric.shape[1]
     chips = n_pair // 2
     box = n == 4 and n_pair == 8
-    parts = n // 2 * aux_dev // (n_pair * chunk_rows)
+    parts = (n - 1) * aux_dev // (n_pair * chunk_rows)
     vmem = pl.BlockSpec(memory_space=pltpu.VMEM)
     smem = pl.BlockSpec(memory_space=pltpu.SMEM)
     dma = pltpu.SemaphoreType.DMA
     hbm = pl.BlockSpec(memory_space=pl.ANY)
     bf16 = jnp.bfloat16
-    scratch = [
-        pltpu.VMEM((chunks, chunk_rows, aux_dev), bf16),
-        pltpu.VMEM((chunks, chunk_rows, aux_dev), bf16),
+    scratch = [pltpu.VMEM((chunks, chunk_rows, aux_dev), bf16) for _ in range(1 if box else 2)] + [
         pltpu.VMEM(metric.shape, bf16),
         dma((3,)),
         pltpu.VMEM((n, chunks, chunk_rows, aux_dev), bf16),
@@ -714,7 +738,7 @@
         scratch += [
             pltpu.VMEM((n_pair, parts, chunk_rows, columns), bf16),
             pltpu.VMEM((chunks, chunk_rows, columns), bf16),
-            dma((chunks,)), dma((chunks,)), dma((2, chunks)), dma((2, chunks)),
+            dma((chunks,)), dma((chunks,)), dma((2, chunks)), dma((2, chunks)), dma((2, chunks)), dma((2, chunks)),
             dma((chunks,)), dma((chunks,)), dma((parts,)), dma((parts,)),
         ]
         for count in (chunks, parts):

time: 78.3 us -> 71.5 us (0.913)
  Pallas kernels: 78 us -> 71.3 us
    pallas_call x1, Pallas kernels: 76 us -> 69.2 us  [per_device(): pl.pallas_call(functools.partial(body, n, n_pair, split), out_shape=(jax....]
where the time goes in v2:
time: 71.5 us; the launch traced here: 71.3 us
  Pallas kernels  71.3 us (100%)
    pallas_call x1, Pallas kernels, per_device(): pl.pallas_call(functools.partial(body, n, n_pair, split), out_shape=(jax....  69.2 us
    pallas_call x1, Pallas kernels, per_device(): pl.pallas_call(functools.partial(close_kernel, width_cw), out_shape=jax.S...  2.06 us

profile of v2, /device:TPU:0, one launch (start us, length us, event | category | flops | bytes accessed | tf_op | source)
XLA Modules:
  0.0 71.3 jit_solution(11497628053437316053)
XLA Ops:
  0.0 69.2 %shard_map.55 = (f32[10,64,256]{2,1,0:T(8,128)}, f32[10,1,256]{2,1,0:T(1,128)}) custom-call(bf16[8,64,512]{2,1,0:T(8,128)(2,1)} %bitcast.2, bf16[2048,512]{1,0:T(8,128)(2,1)} %metric_hbm.1, s32[8,8]{1,0:T(8,128)} %map_ref.1, s32[4,80]{1,0:T(4,128)} %bitcast.3), custom_call_target="tpu_custom_call" | custom-call | tf_op jit(solution)/shard_map/pallas_call | solution.py:758
  69.2 2.1 %shard_map.56 = f32[10,64,256]{2,1,0:T(8,128)} custom-call(f32[10,64,256]{2,1,0:T(8,128)} %get-tuple-element.7.total_ref, f32[10,1,256]{2,1,0:T(1,128)} %get-tuple-element.8.diag_ref, s32[10]{0:T(128)} %cnt_ref.1), custom_call_target="tpu_custom_call" | custom-call | tf_op jit(solution)/shard_map/pallas_call | solution.py:768

commit v3 on v2

--- a/solution.py
+++ b/solution.py
@@ -233,8 +233,8 @@
         diag_copy(k).wait_send()
 
 
-def box_kernel(n, n_pair, split, b_hbm, metric_hbm, map_ref, dom_ref, out_ref, diag_ref,
-               b_raw, metric_ref, in_sem, b_all, table, far_metric, fit_part,
+def box_kernel(n, n_pair, split, b_hbm, metric_hbm, map_hbm, dom_hbm, out_hbm, diag_hbm,
+               map_ref, dom_ref, out_ref, diag_ref, out_sem, b_raw, metric_ref, in_sem, b_all, table, far_metric, fit_part,
                m_s, m_r, o_s, o_r, raw_s, raw_r, w_s, w_r, y_s, y_r,
                tp_s, tp_r, tt_s, tt_r, tf_s, tf_r, mp_s, mp_r, mt_s, mt_r, mf_s, mf_r,
                g_send, g_recv, d_own, d_recv, g_s, g_r, d_s, d_r,
@@ -261,9 +261,13 @@
     load_b = pltpu.make_async_copy(b_hbm.at[0], b_raw.at[0], in_sem.at[0])
     load_rest = pltpu.make_async_copy(b_hbm.at[1:], b_raw.at[1:], in_sem.at[2])
     load_metric = pltpu.make_async_copy(metric_hbm, metric_ref, in_sem.at[1])
+    load_map = pltpu.make_async_copy(map_hbm, map_ref, in_sem.at[3])
+    load_dom = pltpu.make_async_copy(dom_hbm, dom_ref, in_sem.at[4])
+    load_map.start()
     load_b.start()
     load_rest.start()
     load_metric.start()
+    load_dom.start()
     barrier = pltpu.get_barrier_semaphore()
     for there in ((mate, q), (z, partner), (z, near_x), (z, near_y)):
         pl.semaphore_signal(barrier, inc=1, device_id=there, device_id_type=MESH)
@@ -272,6 +276,7 @@
     def _():
         pl.semaphore_signal(barrier, inc=1, device_id=(other, q), device_id_type=MESH)
 
+    load_map.wait()
     aux_blocks = map_ref.shape[1]
     spread_row = lax.broadcasted_iota(jnp.int32, (aux_blocks, depth), 0)
     spread_col = lax.broadcasted_iota(jnp.int32, (aux_blocks, depth), 1) // (depth // aux_blocks)
@@ -522,6 +527,7 @@
         finish(c)
         return carry
 
+    load_dom.wait()
     lax.fori_loop(0, chunks, finish_all, 0)
 
     row_of = lax.broadcasted_iota(jnp.int32, (width, width), 0)
@@ -604,10 +610,55 @@
     def _():
         lax.fori_loop(0, pairs, near_late, 0)
 
+    def drain_all(c, carry):
+        drain(c)
+
+        @pl.when(is_end | (c < whole))
+        def _():
+            swap(c).wait_send()
+
+        @pl.when(is_mid)
+        def _():
+            own(c).wait_send()
+            relay(c).wait_send()
+
+            @pl.when(c < whole)
+            def _():
+                for k in (0, 1):
+                    raw(k, c).wait_send()
+
+            @pl.when(c >= whole)
+            def _():
+                half_fit(c).wait_send()
+        return carry
+
+    lax.fori_loop(0, chunks, drain_all, 0)
+    for t in range(parts):
+        @pl.when(is_end)
+        def _():
+            metric_part(t).wait_send()
+
+        @pl.when(is_mid)
+        def _():
+            m_drain(t)
+
     for mid, below in ((1, True), (2, False)):
         @pl.when(z == mid)
         def _():
             combine(below)
+
+    def leave(p):
+        return pltpu.make_async_copy(out_ref.at[p], out_hbm.at[p], out_sem.at[p])
+
+    leave_diag = pltpu.make_async_copy(diag_ref, diag_hbm, in_sem.at[3])
+    for k in range(1, n):
+        diag_copy(k).wait_recv()
+
+    diag = d_own[...]
+    for k in range(1, n):
+        diag += d_recv[k - 1]
+    diag_ref[...] = diag
+    leave_diag.start()
 
     def add(p, carry):
         remote(g_send.at[0, p], g_recv.at[1, p], g_s.at[0, p], g_r.at[1, p], (mate, q)).wait_recv()
@@ -625,50 +676,15 @@
                 pieces = (late_recv[p], far_recv[p, mid * slab:(mid + 1) * slab])
                 whole = jnp.concatenate(pieces if below else pieces[::-1], axis=1)
                 out_ref[p] = total + whole.astype(jnp.float32)
+
+        leave(p).start()
         return carry
 
     lax.fori_loop(0, pairs, add, 0)
-    for k in range(1, n):
-        diag_copy(k).wait_recv()
-
-    diag = d_own[...]
-    for k in range(1, n):
-        diag += d_recv[k - 1]
-    diag_ref[...] = diag
-
-    def drain_all(c, carry):
-        drain(c)
-
-        @pl.when(is_end | (c < whole))
-        def _():
-            swap(c).wait_send()
-
-        @pl.when(is_mid)
-        def _():
-            own(c).wait_send()
-            relay(c).wait_send()
-
-            @pl.when(c < whole)
-            def _():
-                for k in (0, 1):
-                    raw(k, c).wait_send()
-
-            @pl.when(c >= whole)
-            def _():
-                half_fit(c).wait_send()
-        return carry
-
-    lax.fori_loop(0, chunks, drain_all, 0)
-    for t in range(parts):
-        @pl.when(is_end)
-        def _():
-            metric_part(t).wait_send()
-
-        @pl.when(is_mid)
-        def _():
-            m_drain(t)
 
     def drain_gram(p, carry):
+        leave(p).wait()
+
         @pl.when(is_end)
         def _():
             late(p).wait_send()
@@ -682,6 +698,7 @@
         return carry
 
     lax.fori_loop(0, pairs, drain_gram, 0)
+    leave_diag.wait()
     for k in range(1, n):
         diag_copy(k).wait_send()
 
@@ -722,7 +739,7 @@
     bf16 = jnp.bfloat16
     scratch = [pltpu.VMEM((chunks, chunk_rows, aux_dev), bf16) for _ in range(1 if box else 2)] + [
         pltpu.VMEM(metric.shape, bf16),
-        dma((3,)),
+        dma((5,)),
         pltpu.VMEM((n, chunks, chunk_rows, aux_dev), bf16),
         pltpu.VMEM((n_pair, chunks, chunk_rows, columns), bf16),
     ]
@@ -733,8 +750,17 @@
         pltpu.VMEM((n - 1, pairs, 1, width), jnp.float32),
     ]
     gram_sems = [dma((n - 1, pairs)), dma((n - 1, pairs)), dma((n - 1,)), dma((n - 1,))]
+    specs, outs = [hbm, hbm, vmem, smem], (vmem, vmem)
     if box:
         body = box_kernel
+        specs, outs = [hbm] * 4, (hbm, hbm)
+        scratch = [
+            pltpu.VMEM(aux_map.shape, jnp.int32),
+            pltpu.SMEM((slots, domains.shape[0]), jnp.int32),
+            pltpu.VMEM((pairs, slab, width), jnp.float32),
+            pltpu.VMEM((pairs, 1, width), jnp.float32),
+            dma((pairs,)),
+        ] + scratch
         scratch += [
             pltpu.VMEM((n_pair, parts, chunk_rows, columns), bf16),
             pltpu.VMEM((chunks, chunk_rows, columns), bf16),
@@ -759,8 +785,8 @@
         functools.partial(body, n, n_pair, split),
         out_shape=(jax.ShapeDtypeStruct((pairs, slab, width), jnp.float32),
                    jax.ShapeDtypeStruct((pairs, 1, width), jnp.float32)),
-        in_specs=[hbm, hbm, vmem, smem],
-        out_specs=(vmem, vmem),
+        in_specs=specs,
+        out_specs=outs,
         scratch_shapes=scratch,
         compiler_params=pltpu.CompilerParams(
             collective_id=0, has_side_effects=True, vmem_limit_bytes=60 * 1024 * 1024),

time: 71.5 us -> 70.1 us (0.980)
  Pallas kernels: 71.3 us -> 69.9 us
    pallas_call x1, Pallas kernels: 69.2 us -> 67.8 us  [per_device(): pl.pallas_call(functools.partial(body, n, n_pair, split), out_shape=(jax....]
where the time goes in v3:
time: 70.1 us; the launch traced here: 69.9 us
  Pallas kernels  69.9 us (100%)
    pallas_call x1, Pallas kernels, per_device(): pl.pallas_call(functools.partial(body, n, n_pair, split), out_shape=(jax....  67.8 us
    pallas_call x1, Pallas kernels, per_device(): pl.pallas_call(functools.partial(close_kernel, width_cw), out_shape=jax.S...  2.06 us

profile of v3, /device:TPU:0, one launch (start us, length us, event | category | flops | bytes accessed | tf_op | source)
XLA Modules:
  0.0 69.9 jit_solution(6061068296791125078)
XLA Ops:
  0.0 67.8 %shard_map.55 = (f32[10,64,256]{2,1,0:T(8,128)}, f32[10,1,256]{2,1,0:T(1,128)}) custom-call(bf16[8,64,512]{2,1,0:T(8,128)(2,1)} %bitcast.2, bf16[2048,512]{1,0:T(8,128)(2,1)} %metric_hbm.1, s32[8,8]{1,0:T(8,128)} %map_hbm.1, s32[4,80]{1,0:T(4,128)} %bitcast.3), custom_call_target="tpu_custom_call" | custom-call | tf_op jit(solution)/shard_map/pallas_call | solution.py:784
  67.8 2.1 %shard_map.56 = f32[10,64,256]{2,1,0:T(8,128)} custom-call(f32[10,64,256]{2,1,0:T(8,128)} %get-tuple-element.7.total_ref, f32[10,1,256]{2,1,0:T(1,128)} %get-tuple-element.8.diag_ref, s32[10]{0:T(128)} %cnt_ref.1), custom_call_target="tpu_custom_call" | custom-call | tf_op jit(solution)/shard_map/pallas_call | solution.py:794

commit v4 on v3

--- a/solution.py
+++ b/solution.py
@@ -238,7 +238,7 @@
                m_s, m_r, o_s, o_r, raw_s, raw_r, w_s, w_r, y_s, y_r,
                tp_s, tp_r, tt_s, tt_r, tf_s, tf_r, mp_s, mp_r, mt_s, mt_r, mf_s, mf_r,
                g_send, g_recv, d_own, d_recv, g_s, g_r, d_s, d_r,
-               g_far, far_out, far_recv, far_send, late_send, late_recv, x_s, x_r, c_s):
+               g_far, far_out, far_recv, far_send, v_recv, t_recv, late_send, late_recv, x_s, x_r, c_s):
     chunks, rows, depth = b_hbm.shape
     pairs, slab, width = out_ref.shape
     slots = dom_ref.shape[0]
@@ -541,25 +541,45 @@
     def late(p):
         return remote(late_send.at[p], late_recv.at[p], g_s.at[0, p], g_r.at[0, p], (mate, q))
 
+    lane = lax.broadcasted_iota(jnp.int32, (slab, half), 1)
+    line = lax.broadcasted_iota(jnp.int32, (slab, half), 0)
+    lower = (lane < slab) & (line >= lane)
+
+    def pack(square):
+        return jnp.where(lower, pltpu.roll(square[slab:], slab, 1), square[:slab])
+
     def to_mid(p):
         return remote(far_out.at[p], far_recv.at[p], x_s.at[p], x_r.at[p], (mate, q))
 
     def across(j, p):
-        return remote(far_send.at[j, p], g_recv.at[1, p], c_s.at[j, p], g_r.at[1, p],
+        return remote(far_send.at[j, p], v_recv.at[p], c_s.at[j, p], g_r.at[1, p],
                       (jnp.where(z < 2, 2, 0) + j, q))
+
+    def packed(p):
+        return remote(far_send.at[2, p], t_recv.at[p], c_s.at[2, p], g_r.at[2, p], (other, q))
+
+    def packed_on(p):
+        return remote(t_recv.at[p], t_recv.at[p], g_s.at[1, p], g_r.at[2, p], (mate, q))
 
     def combine(below):
         def one(p, carry):
             to_mid(p).wait_recv()
-            top = far_recv[p, 0:half].astype(jnp.float32)
-            bottom = far_recv[p, half:width].astype(jnp.float32)
-            parts = (top.T, bottom) if below else (top, bottom.T)
-            value = (g_far[p] + jnp.concatenate(parts, axis=1)).astype(far_send.dtype)
+            far_send[2, p] = (g_far[p, half:] + far_recv[p, half:].astype(jnp.float32)).astype(far_send.dtype)
+            packed(p).start()
+            value = (g_far[p, 0:half] + far_recv[p, 0:half].astype(jnp.float32).T).astype(far_send.dtype)
             for j in ((1, 0) if below else (0, 1)):
                 far_send[j, p] = value[j * slab:(j + 1) * slab]
                 across(j, p).start()
+
+            @pl.when(p >= 2)
+            def _():
+                packed(p - 2).wait_recv()
+                packed_on(p - 2).start()
             return carry
         lax.fori_loop(0, pairs, one, 0)
+        for p in (pairs - 2, pairs - 1):
+            packed(p).wait_recv()
+            packed_on(p).start()
 
     def near_late(p, carry):
         late(p).start()
@@ -588,13 +608,15 @@
 
             @pl.when(z == end)
             def _():
-                far_out[p] = full[:, far_cols].astype(far_out.dtype)
+                far_out[p, 0:half] = full[near_cols, far_cols].astype(far_out.dtype)
+                far_out[p, half:] = pack(full[far_cols, far_cols]).astype(far_out.dtype)
                 late_send[p] = full[mid * slab:(mid + 1) * slab, near_cols].astype(late_send.dtype)
                 to_mid(p).start()
 
             @pl.when(z == mid)
             def _():
-                g_far[p] = full[far_cols]
+                g_far[p, 0:half] = full[far_cols, near_cols]
+                g_far[p, half:] = pack(full[far_cols, far_cols])
                 g_send[0, p] = full[end * slab:(end + 1) * slab].astype(g_send.dtype)
                 near(p).start()
         return carry
@@ -661,21 +683,32 @@
     leave_diag.start()
 
     def add(p, carry):
-        remote(g_send.at[0, p], g_recv.at[1, p], g_s.at[0, p], g_r.at[1, p], (mate, q)).wait_recv()
-        total = out_ref[p] + g_recv[1, p].astype(jnp.float32)
+        across(0, p).wait_recv()
 
         @pl.when(is_end)
         def _():
-            near(p).wait_recv()
-            out_ref[p] = total + g_recv[0, p].astype(jnp.float32)
-
-        for mid, below in ((1, True), (2, False)):
-            @pl.when(z == mid)
-            def _():
-                late(p).wait_recv()
-                pieces = (late_recv[p], far_recv[p, mid * slab:(mid + 1) * slab])
-                whole = jnp.concatenate(pieces if below else pieces[::-1], axis=1)
-                out_ref[p] = total + whole.astype(jnp.float32)
+            packed(p).wait_recv()
+
+        tied = t_recv[p].astype(jnp.float32)
+        twice = jnp.concatenate((tied, tied), axis=0).T
+        cross = v_recv[p].astype(jnp.float32)
+        for d in range(n):
+            @pl.when(z == d)
+            def _():
+                if d % 2 == 0:
+                    side = jnp.where(lower, twice[:slab], tied)
+                else:
+                    side = jnp.where(line < lane - slab, twice[:slab], pltpu.roll(tied, slab, 1))
+                    side = jnp.where(lane < slab, twice[slab:], side)
+                total = out_ref[p] + jnp.concatenate((side, cross) if d < 2 else (cross, side), axis=1)
+                if d in (0, n - 1):
+                    near(p).wait_recv()
+                    out_ref[p] = total + g_recv[0, p].astype(jnp.float32)
+                else:
+                    late(p).wait_recv()
+                    pieces = (late_recv[p], far_recv[p, d % 2 * slab:(d % 2 + 1) * slab])
+                    whole_row = jnp.concatenate(pieces if d < 2 else pieces[::-1], axis=1)
+                    out_ref[p] = total + whole_row.astype(jnp.float32)
 
         leave(p).start()
         return carry
@@ -695,6 +728,8 @@
             near(p).wait_send()
             for j in range(2):
                 across(j, p).wait_send()
+            packed(p).wait_send()
+            packed_on(p).wait_send()
         return carry
 
     lax.fori_loop(0, pairs, drain_gram, 0)
@@ -745,7 +780,7 @@
     ]
     grams = [
         pltpu.VMEM((1 if box else n, pairs, slab, width), bf16),
-        pltpu.VMEM((2 if box else n - 1, pairs, slab, width), bf16),
+        pltpu.VMEM((1 if box else n - 1, pairs, slab, width), bf16),
         pltpu.VMEM((pairs, 1, width), jnp.float32),
         pltpu.VMEM((n - 1, pairs, 1, width), jnp.float32),
     ]
@@ -770,13 +805,15 @@
         for count in (chunks, parts):
             scratch += [dma((k, count)) for k in (3, 3, 2, 2, 3, 3)]
         scratch += grams + gram_sems + [
-            pltpu.VMEM((pairs, width // 2, width), jnp.float32),
-            pltpu.VMEM((pairs, width, width // 2), bf16),
-            pltpu.VMEM((pairs, width, width // 2), bf16),
-            pltpu.VMEM((2, pairs, slab, width), bf16),
+            pltpu.VMEM((pairs, width - slab, width // 2), jnp.float32),
+            pltpu.VMEM((pairs, width - slab, width // 2), bf16),
+            pltpu.VMEM((pairs, width - slab, width // 2), bf16),
+            pltpu.VMEM((3, pairs, slab, width // 2), bf16),
             pltpu.VMEM((pairs, slab, width // 2), bf16),
             pltpu.VMEM((pairs, slab, width // 2), bf16),
-            dma((pairs,)), dma((pairs,)), dma((2, pairs)),
+            pltpu.VMEM((pairs, slab, width // 2), bf16),
+            pltpu.VMEM((pairs, slab, width // 2), bf16),
+            dma((pairs,)), dma((pairs,)), dma((3, pairs)),
         ]
     else:
         body = line_kernel

time: 70.1 us -> 68.7 us (0.980)
  Pallas kernels: 69.9 us -> 68.5 us
    pallas_call x1, Pallas kernels: 67.8 us -> 66.4 us  [per_device(): pl.pallas_call(functools.partial(body, n, n_pair, split), out_shape=(jax....]
where the time goes in v4:
time: 68.7 us; the launch traced here: 68.5 us
  Pallas kernels  68.5 us (100%)
    pallas_call x1, Pallas kernels, per_device(): pl.pallas_call(functools.partial(body, n, n_pair, split), out_shape=(jax....  66.4 us
    pallas_call x1, Pallas kernels, per_device(): pl.pallas_call(functools.partial(close_kernel, width_cw), out_shape=jax.S...  2.06 us

profile of v4, /device:TPU:0, one launch (start us, length us, event | category | flops | bytes accessed | tf_op | source)
XLA Modules:
  0.0 68.5 jit_solution(17934194223250093492)
XLA Ops:
  0.0 66.4 %shard_map.55 = (f32[10,64,256]{2,1,0:T(8,128)}, f32[10,1,256]{2,1,0:T(1,128)}) custom-call(bf16[8,64,512]{2,1,0:T(8,128)(2,1)} %bitcast.2, bf16[2048,512]{1,0:T(8,128)(2,1)} %metric_hbm.1, s32[8,8]{1,0:T(8,128)} %map_hbm.1, s32[4,80]{1,0:T(4,128)} %bitcast.3), custom_call_target="tpu_custom_call" | custom-call | tf_op jit(solution)/shard_map/pallas_call | solution.py:821
  66.5 2.1 %shard_map.56 = f32[10,64,256]{2,1,0:T(8,128)} custom-call(f32[10,64,256]{2,1,0:T(8,128)} %get-tuple-element.7.total_ref, f32[10,1,256]{2,1,0:T(1,128)} %get-tuple-element.8.diag_ref, s32[10]{0:T(128)} %cnt_ref.1), custom_call_target="tpu_custom_call" | custom-call | tf_op jit(solution)/shard_map/pallas_call | solution.py:831
